TPU v7x, 256 devices: a whole 4x4x8 slice. The times are simulated.
256 devices in a mesh: row: 16 (over z, core), col: 8 (over x_hi, y), feat: 2 (over x_lo).
Axes of the slice: x: 4 (x_hi: 2, x_lo: 2; x = x_hi * 2 + x_lo), y: 4, z: 8, core: 2. Of those that a mesh axis runs over, the one named last changes fastest.
Arguments:
- features: bfloat16 [65536, 256], P(('col', 'row'), 'feat'), may hold values from -6 to 6
- tile_rows: int32 [16, 8, 256], P('row', 'col'), may hold values from 0 to 31, as said below
- tile_cols: int32 [16, 8, 256], P('row', 'col'), may hold values from 0 to 63
- tile_count: int32 [16, 8], P('row', 'col'), may hold values from 64 to 256, as said below
- tile_values: bfloat16 [16, 8, 256, 128, 128], P('row', 'col'), may hold values from -0.21875 to 0.21875
- weights: bfloat16 [256, 256], replicated, may hold values from -0.375 to 0.375
- cotangent: bfloat16 [65536, 256], P(('row', 'col'), 'feat'), may hold values from -6 to 6
Outputs:
- activated: bfloat16 [65536, 256], P(('row', 'col'), 'feat')
- feature_grad: bfloat16 [65536, 256], P(('col', 'row'), 'feat')
- weight_grad: float32 [256, 256], P('feat')
Inputs may be any that keep to these rules, and one draw needn't show every extreme that they name: `tile_rows`: block rows of a cell, unevenly loaded. `tile_count`: some cell has all 256 slots live.
All inputs are finite; a program needn't handle non-finite values.
Results may differ from a plain program's by a relative error of at most 0.027.
Values may be sent and summed in bfloat16 or wider, within the bound.
A program may use at most 128 MiB of HBM per device.

v0:
```python
import jax
import jax.numpy as jnp
from jax import lax
from jax.sharding import PartitionSpec as P


def shards(features, tile_rows, tile_cols, tile_count, tile_values, weights, cotangent):
    width = tile_values.shape[-1]
    slots = tile_values.shape[2]
    local_tiles = tile_values[0, 0]
    block_rows = tile_rows[0, 0]
    block_cols = tile_cols[0, 0]
    live_mask = (jnp.arange(slots) < tile_count[0, 0]).astype(jnp.float32)
    n_rowdev = lax.axis_size("row")
    n_coldev = lax.axis_size("col")
    local_blocks = features.shape[0] // width
    feat_half = features.shape[1]
    feat_index = lax.axis_index("feat")
    row_blocks = local_blocks * n_coldev
    col_blocks = local_blocks * n_rowdev
    node_total = features.shape[0] * n_rowdev * n_coldev
    panel = lax.all_gather(features, "row", axis=0, tiled=True)
    gathered = panel.reshape(col_blocks, width, feat_half)[block_cols]
    products = jnp.einsum("tij,tjf->tif", local_tiles, gathered, preferred_element_type=jnp.float32)
    products = products * live_mask[:, None, None]
    partial_value = (
        jnp.zeros((row_blocks, width, feat_half), jnp.float32).at[block_rows].add(products)
    )
    summed = lax.psum_scatter(
        partial_value.reshape(row_blocks * width, feat_half).astype(jnp.bfloat16),
        "col",
        scatter_dimension=0,
        tiled=True,
    )
    weight_rows = lax.dynamic_slice_in_dim(weights, feat_index * feat_half, feat_half, 0)
    mix_term = jnp.dot(summed, weight_rows, preferred_element_type=jnp.float32)
    hidden = lax.psum_scatter(
        mix_term.astype(jnp.bfloat16), "feat", scatter_dimension=1, tiled=True
    ).astype(jnp.float32)
    negative = jnp.minimum(hidden, 0.0)
    activated = jnp.where(hidden > 0, hidden, jnp.expm1(negative)).astype(jnp.bfloat16)
    slope_factor = jnp.where(hidden > 0, 1.0, jnp.exp(negative))
    grad_out = (cotangent.astype(jnp.float32) * slope_factor).astype(jnp.bfloat16)
    grad_whole = lax.all_gather(grad_out, "feat", axis=1, tiled=True)
    weight_term = lax.dot_general(
        summed, grad_whole, (((0,), (0,)), ((), ())), preferred_element_type=jnp.float32
    )
    n_feat = lax.axis_size("feat")
    slots = jnp.zeros((n_feat,) + weight_term.shape, jnp.float32)
    slots = lax.dynamic_update_slice_in_dim(slots, weight_term[None], feat_index, 0)
    slots = lax.psum(slots, ("row", "col", "feat"))
    weight_grad = lax.dynamic_index_in_dim(slots, feat_index, 0, keepdims=False) * node_total ** (
        -0.5
    )
    spread = lax.dot_general(
        grad_whole, weight_rows, (((1,), (1,)), ((), ())), preferred_element_type=jnp.float32
    ).astype(jnp.bfloat16)
    spread_panel = lax.all_gather(spread, "col", axis=0, tiled=True)
    spread_blocks = spread_panel.reshape(row_blocks, width, feat_half)[block_rows]
    back_products = jnp.einsum(
        "tji,tjf->tif", local_tiles, spread_blocks, preferred_element_type=jnp.float32
    )
    back_products = back_products * live_mask[:, None, None]
    back_partial = (
        jnp.zeros((col_blocks, width, feat_half), jnp.float32).at[block_cols].add(back_products)
    )
    back_summed = lax.psum_scatter(
        back_partial.reshape(col_blocks * width, feat_half).astype(jnp.bfloat16),
        "row",
        scatter_dimension=0,
        tiled=True,
    )
    return (activated, back_summed, weight_grad)


def solution(mesh):
    return jax.shard_map(
        shards,
        mesh=mesh,
        in_specs=(
            P(("col", "row"), "feat"),
            P("row", "col", None),
            P("row", "col", None),
            P("row", "col"),
            P("row", "col", None, None, None),
            P(),
            P(("row", "col"), "feat"),
        ),
        out_specs=(P(("row", "col"), "feat"), P(("col", "row"), "feat"), P("feat", None)),
        check_vma=False,
    )
```

profile of v0, /device:TPU:2, one launch (start us, length us, event | category | flops | bytes accessed | tf_op | source)
XLA Modules:
  0.0 605.1 jit_solution(15216501221385841070)
XLA Ops:
  9.3 43.2 %all-gather.3.cloned.1.call-done = bf16[8192,128]{1,0:T(8,128)(2,1)} async-done(((bf16[512,128]{1,0:T(8,128)(2,1)}), bf16[8192,128]{1,0:T(8,128)(2,1)}) %all-gather.3.cloned.1.call-update) | async-done | bytes 2097168 | tf_op jit(solution)/shard_map/all_gather | solution.py:22
  52.6 10.2 %gather_fusion = bf16[256,128,128]{2,1,0:T(8,128)(2,1)} fusion(bf16[64,128,128]{2,1,0:T(8,128)(2,1)} %bitcast.36, s32[1024]{0:T(1024)S(1)} %pad_clamp_fusion.1), kind=kCustom, calls=%fused_computation | custom fusion | bytes 16778240 | tf_op jit(solution)/shard_map/gather | solution.py:23
  62.8 13.0 %multiply_bitcast_fusion.1 = f32[256,128,128]{1,2,0:T(8,128)} fusion(bf16[256,128,128]{2,1,0:T(8,128)(2,1)} %gather_fusion, bf16[1,1,256,128,128]{4,3,2,1,0:T(8,128)(2,1)} %param.11, f32[256]{0:T(256)S(1)} %compare_convert_fusion), kind=kOutput, calls=%fused_computation.5 | convolution fusion | flops 1077936128 | bytes 33555456 | tf_op jit(solution)/shard_map/tij,tjf->tif/dot_general | solution.py:24
  75.8 17.4 %copy.17 = f32[256,128,128]{2,1,0:T(8,128)} copy(f32[256,128,128]{1,2,0:T(8,128)} %multiply_bitcast_fusion.1) | data formatting | bytes 33554432 | tf_op jit(solution)/shard_map/mul | solution.py:25
  93.5 33.2 %scatter_fusion = f32[32,128,128]{2,1,0:T(8,128)S(1)} fusion(f32[32,128,128]{2,1,0:T(8,128)S(1)} %broadcast_in_dim.22, s32[256]{0:T(256)S(1)} %bitcast.43, f32[256,128,128]{2,1,0:T(8,128)} %copy.17), kind=kCustom, calls=%fused_computation.2 | custom fusion | flops 4194304 | bytes 50332672 | tf_op jit(solution)/shard_map/scatter-add | solution.py:27
  126.7 1.1 convert_element_type.38
  127.9 74.5 %reduce-scatter.6.cloned.1.call-done = bf16[512,128]{1,0:T(8,128)(2,1)} async-done(((bf16[4096,128]{1,0:T(8,128)(2,1)}), bf16[512,128]{1,0:T(8,128)(2,1)}) %reduce-scatter.6.cloned.1.call-update) | async-done | bytes 131088 | tf_op jit(solution)/shard_map/reduce_scatter | solution.py:29
  202.4 1.1 convolution_convert_fusion
  203.5 0.8 copy.22
  204.4 16.0 %reduce-scatter.10.cloned.1.call-done = bf16[128,512]{1,0:T(8,128)(2,1)} async-done(((bf16[256,512]{1,0:T(8,128)(2,1)}), bf16[128,512]{1,0:T(8,128)(2,1)}) %reduce-scatter.10.cloned.1.call-update) | async-done | bytes 131088
  220.4 1.0 copy.23
  222.3 5.9 all_gather.10
  228.2 0.9 convolution_convert_fusion.1
  229.2 1.1 fusion.2
  231.3 50.6 %all-gather.5.cloned.1.call-done = bf16[4096,128]{1,0:T(8,128)(2,1)} async-done(((bf16[512,128]{1,0:T(8,128)(2,1)}), bf16[4096,128]{1,0:T(8,128)(2,1)}) %all-gather.5.cloned.1.call-update) | async-done | bytes 1048592 | tf_op jit(solution)/shard_map/all_gather | solution.py:58
  281.9 9.8 %gather_fusion.1 = bf16[256,128,128]{2,1,0:T(8,128)(2,1)} fusion(bf16[32,128,128]{2,1,0:T(8,128)(2,1)} %bitcast.35, s32[1024]{0:T(1024)S(1)} %pad_clamp_fusion), kind=kCustom, calls=%fused_computation.1 | custom fusion | bytes 16778240 | tf_op jit(solution)/shard_map/gather | solution.py:59
  291.7 15.4 %multiply_bitcast_fusion = f32[256,128,128]{1,2,0:T(8,128)} fusion(bf16[256,128,128]{2,1,0:T(8,128)(2,1)} %gather_fusion.1, bf16[1,1,256,128,128]{4,3,2,1,0:T(8,128)(2,1)} %param.11, f32[256]{0:T(256)S(1)} %compare_convert_fusion), kind=kOutput, calls=%fused_computation.4 | convolution fusion | flops 1077936128 | bytes 33555456 | tf_op jit(solution)/shard_map/tji,tjf->tif/dot_general | solution.py:60
  307.1 17.5 %copy.19 = f32[256,128,128]{2,1,0:T(8,128)} copy(f32[256,128,128]{1,2,0:T(8,128)} %multiply_bitcast_fusion) | data formatting | bytes 33554432 | tf_op jit(solution)/shard_map/mul | solution.py:63
  324.6 2.5 broadcast_in_dim.23
  327.0 52.1 %scatter_fusion.1 = f32[64,128,128]{2,1,0:T(8,128)} fusion(f32[64,128,128]{2,1,0:T(8,128)} %broadcast_in_dim.23, s32[256]{0:T(256)S(1)} %bitcast.42, f32[256,128,128]{2,1,0:T(8,128)} %copy.19), kind=kCustom, calls=%fused_computation.3 | custom fusion | flops 4194304 | bytes 50332672 | tf_op jit(solution)/shard_map/scatter-add | solution.py:65
  379.1 3.9 convert_element_type.46
  383.1 154.2 %all-reduce.2.cloned.1.call-done = f32[2,128,256]{2,1,0:T(8,128)} async-done(((f32[2,128,256]{2,1,0:T(8,128)}), f32[2,128,256]{2,1,0:T(8,128)}) %all-reduce.2.cloned.1.call-update) | async-done | bytes 262160 | tf_op jit(solution)/shard_map/psum | solution.py:51
  537.3 1.6 multiply_bitcast_fusion.2
  538.8 59.4 %reduce-scatter.8.cloned.1.call-done = bf16[512,128]{1,0:T(8,128)(2,1)} async-done(((bf16[8192,128]{1,0:T(8,128)(2,1)}), bf16[512,128]{1,0:T(8,128)(2,1)}) %reduce-scatter.8.cloned.1.call-update) | async-done | bytes 131088 | tf_op jit(solution)/shard_map/reduce_scatter | solution.py:67
  (27 shorter events, 3.7 us)
Async XLA Ops:
  7.2 195.2 %copy-start = (bf16[256,256]{1,0:T(8,128)(2,1)S(1)}, bf16[256,256]{1,0:T(8,128)(2,1)}, u32[]{:S(2)}) copy-start(bf16[256,256]{1,0:T(8,128)(2,1)} %param.12) | copy-start | bytes 393220
  7.2 45.4 %all-gather.3.cloned.1.call-start = ((), (), s32[]{:S(2)}) async-start(), calls=%async_computation.3 | async-start | bytes 2228224 | tf_op jit(solution)/shard_map/all_gather | solution.py:22
  7.9 194.4 %reduce-scatter.6.cloned.1.call-start = ((), (), s32[]{:S(2)}) async-start(), calls=%async_computation.4 | async-start | bytes 1179648 | tf_op jit(solution)/shard_map/reduce_scatter | solution.py:29
  93.5 128.0 %copy-start.3 = (bf16[512,128]{1,0:T(8,128)(2,1)S(1)}, bf16[512,128]{1,0:T(8,128)(2,1)}, u32[]{:S(2)}) copy-start(bf16[512,128]{1,0:T(8,128)(2,1)} %param.13) | copy-start | bytes 393220
  127.8 92.6 %reduce-scatter.10.cloned.1.call-start = ((), (), s32[]{:S(2)}) async-start(), calls=%async_computation.8 | async-start | bytes 393216
  204.3 77.5 %all-gather.5.cloned.1.call-start = ((), (), s32[]{:S(2)}) async-start(), calls=%async_computation.5 | async-start | bytes 1179648 | tf_op jit(solution)/shard_map/all_gather | solution.py:58
  229.1 308.2 %all-reduce.2.cloned.1.call-start = ((), (), s32[]{:S(2)}) async-start(), calls=%async_computation.7 | async-start | bytes 524288 | tf_op jit(solution)/shard_map/psum | solution.py:51
  230.3 0.7 copy-start.2
  231.0 367.2 %reduce-scatter.8.cloned.1.call-start = ((), (), s32[]{:S(2)}) async-start(), calls=%async_computation.6 | async-start | bytes 2228224 | tf_op jit(solution)/shard_map/reduce_scatter | solution.py:67
  327.0 271.2 %copy-start.1 = (bf16[256,256]{1,0:T(8,128)(2,1)S(1)}, bf16[256,256]{1,0:T(8,128)(2,1)}, u32[]{:S(2)}) copy-start(bf16[256,256]{1,0:T(8,128)(2,1)} %param.12) | copy-start | bytes 393220
Sparse Core Ops, SparseCore 0:
  9.8 42.6 all-gather.2
  127.9 74.3 reduce-scatter.5
  205.0 15.3 reduce-scatter.9
  229.2 52.6 all-gather.4
  287.2 250.0 all-reduce.1
  540.2 57.9 reduce-scatter.7
where the time goes:
time: 607 us; the launch traced here: 605 us
  waiting for transfers between devices  399 us (66%)
  other arithmetic  93.4 us (15%)
  local copies, waits for them, and re-layouts  60.2 us (10%)
  matrix products  31.5 us (5%)
  between operations  14.9 us (2%)
    psum x1, waiting for transfers between devices, shards(): slots = lax.psum(slots, ('row', 'col', 'feat'))  154 us
    reduce_scatter x1, waiting for transfers between devices, shards(): lax.psum_scatter(partial_value.reshape(row_blocks * width, feat_half).ast...  74.5 us
    reduce_scatter x1, waiting for transfers between devices, shards(): lax.psum_scatter(back_partial.reshape(col_blocks * width, feat_half).asty...  59.4 us
    scatter-add x1, other arithmetic, shards(): jnp.zeros((col_blocks, width, feat_half), jnp.float32).at[block_cols]  52.1 us
    all_gather x1, waiting for transfers between devices, shards(): spread_panel = lax.all_gather(spread, 'col', axis=0, tiled=True)  50.6 us
    all_gather x1, waiting for transfers between devices, shards(): panel = lax.all_gather(features, 'row', axis=0, tiled=True)  43.2 us
    scatter-add x1, other arithmetic, shards(): jnp.zeros((row_blocks, width, feat_half), jnp.float32).at[block_rows]  33.2 us
    mul x1, local copies, waits for them, and re-layouts, shards(): back_products = back_products * live_mask[:, None, None]  17.5 us
  transfers between devices with their start and end apart: 6, of which 6 were waited for; matrix products, arithmetic and copies ran while one was open for 17% of the time, Pallas kernels for 0%

commit v1 on v0

--- a/solution.py
+++ b/solution.py
@@ -48,7 +48,8 @@
     n_feat = lax.axis_size("feat")
     slots = jnp.zeros((n_feat,) + weight_term.shape, jnp.float32)
     slots = lax.dynamic_update_slice_in_dim(slots, weight_term[None], feat_index, 0)
-    slots = lax.psum(slots, ("row", "col", "feat"))
+    parts = lax.all_gather(slots, ("row", "col", "feat"))
+    slots = jnp.sum(parts, axis=0)
     weight_grad = lax.dynamic_index_in_dim(slots, feat_index, 0, keepdims=False) * node_total ** (
         -0.5
     )

time: 607 us -> 1150 us (1.89)
  waiting for transfers between devices: 399 us -> 923 us
  other arithmetic: 93.4 us -> 114 us
    all_gather x0 -> x1, waiting for transfers between devices: none -> 695 us  [shards(): parts = lax.all_gather(slots, ('row', 'col', 'feat'))]
    psum x1 -> x0, waiting for transfers between devices: 154 us -> none  [shards(): slots = lax.psum(slots, ('row', 'col', 'feat'))]
    reduce_sum x0 -> x1, other arithmetic: none -> 21.2 us  [shards(): slots = jnp.sum(parts, axis=0)]
    reduce_scatter x1, waiting for transfers between devices: 59.4 us -> 43.4 us  [shards(): lax.psum_scatter(back_partial.reshape(col_blocks * width, feat_half).asty...]
  transfers between devices with their start and end apart: 6 -> 6, of which waited for: 6 -> 6; matrix products, arithmetic and copies ran while one was open for 17% -> 11% of each run, Pallas kernels for 0% -> 0%
where the time goes in v1:
time: 1150 us
  waiting for transfers between devices  923 us (80%)
  other arithmetic  114 us (10%)
  local copies, waits for them, and re-layouts  60.3 us (5%)
  matrix products  31.7 us (3%)
  between operations  14.9 us (1%)
    all_gather x1, waiting for transfers between devices, shards(): parts = lax.all_gather(slots, ('row', 'col', 'feat'))  695 us
    reduce_scatter x1, waiting for transfers between devices, shards(): lax.psum_scatter(partial_value.reshape(row_blocks * width, feat_half).ast...  74.5 us
    scatter-add x1, other arithmetic, shards(): jnp.zeros((col_blocks, width, feat_half), jnp.float32).at[block_cols]  52.3 us
    all_gather x1, waiting for transfers between devices, shards(): spread_panel = lax.all_gather(spread, 'col', axis=0, tiled=True)  50.6 us
    reduce_scatter x1, waiting for transfers between devices, shards(): lax.psum_scatter(back_partial.reshape(col_blocks * width, feat_half).asty...  43.4 us
    all_gather x1, waiting for transfers between devices, shards(): panel = lax.all_gather(features, 'row', axis=0, tiled=True)  43.2 us
    scatter-add x1, other arithmetic, shards(): jnp.zeros((row_blocks, width, feat_half), jnp.float32).at[block_rows]  33.2 us
  transfers between devices with their start and end apart: 6, of which 6 were waited for; matrix products, arithmetic and copies ran while one was open for 11% of the time, Pallas kernels for 0%

profile of v1, /device:TPU:2, one launch (start us, length us, event | category | flops | bytes accessed | tf_op | source)
XLA Modules:
  0.0 1150.6 jit_solution(13731714298730656000)
XLA Ops:
  9.3 43.2 %all-gather.4.cloned.1.call-done = bf16[8192,128]{1,0:T(8,128)(2,1)} async-done(((bf16[512,128]{1,0:T(8,128)(2,1)}), bf16[8192,128]{1,0:T(8,128)(2,1)}) %all-gather.4.cloned.1.call-update) | async-done | bytes 2097168 | tf_op jit(solution)/shard_map/all_gather | solution.py:22
  52.6 10.2 gather_fusion
  62.8 13.0 %multiply_bitcast_fusion.1 = f32[256,128,128]{1,2,0:T(8,128)} fusion(bf16[256,128,128]{2,1,0:T(8,128)(2,1)} %gather_fusion, bf16[1,1,256,128,128]{4,3,2,1,0:T(8,128)(2,1)} %param.11, f32[256]{0:T(256)S(1)} %compare_convert_fusion), kind=kOutput, calls=%fused_computation.5 | convolution fusion | flops 1077936128 | bytes 33555456 | tf_op jit(solution)/shard_map/tij,tjf->tif/dot_general | solution.py:24
  75.8 17.4 %copy.17 = f32[256,128,128]{2,1,0:T(8,128)} copy(f32[256,128,128]{1,2,0:T(8,128)} %multiply_bitcast_fusion.1) | data formatting | bytes 33554432 | tf_op jit(solution)/shard_map/mul | solution.py:25
  93.5 33.2 %scatter_fusion = f32[32,128,128]{2,1,0:T(8,128)S(1)} fusion(f32[32,128,128]{2,1,0:T(8,128)S(1)} %broadcast_in_dim.10, s32[256]{0:T(256)S(1)} %bitcast.43, f32[256,128,128]{2,1,0:T(8,128)} %copy.17), kind=kCustom, calls=%fused_computation.2 | custom fusion | flops 4194304 | bytes 50332672 | tf_op jit(solution)/shard_map/scatter-add | solution.py:27
  126.7 1.1 convert_element_type.38
  127.9 74.5 %reduce-scatter.6.cloned.1.call-done = bf16[512,128]{1,0:T(8,128)(2,1)} async-done(((bf16[4096,128]{1,0:T(8,128)(2,1)}), bf16[512,128]{1,0:T(8,128)(2,1)}) %reduce-scatter.6.cloned.1.call-update) | async-done | bytes 131088 | tf_op jit(solution)/shard_map/reduce_scatter | solution.py:29
  202.4 1.1 convolution_convert_fusion
  203.5 0.8 copy.22
  204.4 16.0 %reduce-scatter.10.cloned.1.call-done = bf16[128,512]{1,0:T(8,128)(2,1)} async-done(((bf16[256,512]{1,0:T(8,128)(2,1)}), bf16[128,512]{1,0:T(8,128)(2,1)}) %reduce-scatter.10.cloned.1.call-update) | async-done | bytes 131088
  220.4 1.0 copy.23
  222.3 5.9 all_gather.16
  228.2 0.9 convolution_convert_fusion.1
  229.1 1.1 fusion.2
  231.3 50.6 %all-gather.6.cloned.1.call-done = bf16[4096,128]{1,0:T(8,128)(2,1)} async-done(((bf16[512,128]{1,0:T(8,128)(2,1)}), bf16[4096,128]{1,0:T(8,128)(2,1)}) %all-gather.6.cloned.1.call-update) | async-done | bytes 1048592 | tf_op jit(solution)/shard_map/all_gather | solution.py:59
  281.9 9.8 gather_fusion.1
  291.7 15.6 %multiply_bitcast_fusion = f32[256,128,128]{1,2,0:T(8,128)} fusion(bf16[256,128,128]{2,1,0:T(8,128)(2,1)} %gather_fusion.1, bf16[1,1,256,128,128]{4,3,2,1,0:T(8,128)(2,1)} %param.11, f32[256]{0:T(256)S(1)} %compare_convert_fusion), kind=kOutput, calls=%fused_computation.4 | convolution fusion | flops 1077936128 | bytes 33555456 | tf_op jit(solution)/shard_map/tji,tjf->tif/dot_general | solution.py:61
  307.3 17.5 %copy.19 = f32[256,128,128]{2,1,0:T(8,128)} copy(f32[256,128,128]{1,2,0:T(8,128)} %multiply_bitcast_fusion) | data formatting | bytes 33554432 | tf_op jit(solution)/shard_map/mul | solution.py:64
  324.8 2.5 broadcast_in_dim.11
  327.3 52.3 %scatter_fusion.1 = f32[64,128,128]{2,1,0:T(8,128)} fusion(f32[64,128,128]{2,1,0:T(8,128)} %broadcast_in_dim.11, s32[256]{0:T(256)S(1)} %bitcast.42, f32[256,128,128]{2,1,0:T(8,128)} %copy.19), kind=kCustom, calls=%fused_computation.3 | custom fusion | flops 4194304 | bytes 50332672 | tf_op jit(solution)/shard_map/scatter-add | solution.py:66
  379.6 3.9 convert_element_type.46
  383.5 695.0 %all-gather.8.cloned.1.call-done = f32[256,2,128,256]{3,2,1,0:T(8,128)} async-done(((f32[1,2,128,256]{3,2,1,0:T(8,128)}), f32[256,2,128,256]{3,2,1,0:T(8,128)}) %all-gather.8.cloned.1.call-update) | async-done | bytes 67108880 | tf_op jit(solution)/shard_map/all_gather | solution.py:51
  1078.5 21.2 %reduce_sum.9 = f32[2,128,256]{2,1,0:T(8,128)S(1)} reduce(f32[256,2,128,256]{3,2,1,0:T(8,128)} %all-gather.8.cloned.1.call-done, f32[]{:T(128)} %constant.10.clone.1), dimensions={0}, to_apply=%region_5.6 | reduce | flops 16711680 | bytes 67371008 | tf_op jit(solution)/shard_map/reduce_sum | solution.py:52
  1100.4 43.4 %reduce-scatter.8.cloned.1.call-done = bf16[512,128]{1,0:T(8,128)(2,1)} async-done(((bf16[8192,128]{1,0:T(8,128)(2,1)}), bf16[512,128]{1,0:T(8,128)(2,1)}) %reduce-scatter.8.cloned.1.call-update) | async-done | bytes 131088 | tf_op jit(solution)/shard_map/reduce_scatter | solution.py:68
  (28 shorter events, 4.3 us)
Async XLA Ops:
  7.2 195.2 %copy-start = (bf16[256,256]{1,0:T(8,128)(2,1)S(1)}, bf16[256,256]{1,0:T(8,128)(2,1)}, u32[]{:S(2)}) copy-start(bf16[256,256]{1,0:T(8,128)(2,1)} %param.12) | copy-start | bytes 393220
  7.2 45.4 %all-gather.4.cloned.1.call-start = ((), (), s32[]{:S(2)}) async-start(), calls=%async_computation.3 | async-start | bytes 2228224 | tf_op jit(solution)/shard_map/all_gather | solution.py:22
  7.9 194.4 %reduce-scatter.6.cloned.1.call-start = ((), (), s32[]{:S(2)}) async-start(), calls=%async_computation.4 | async-start | bytes 1179648 | tf_op jit(solution)/shard_map/reduce_scatter | solution.py:29
  93.5 128.0 %copy-start.3 = (bf16[512,128]{1,0:T(8,128)(2,1)S(1)}, bf16[512,128]{1,0:T(8,128)(2,1)}, u32[]{:S(2)}) copy-start(bf16[512,128]{1,0:T(8,128)(2,1)} %param.13) | copy-start | bytes 393220
  127.8 92.6 %reduce-scatter.10.cloned.1.call-start = ((), (), s32[]{:S(2)}) async-start(), calls=%async_computation.8 | async-start | bytes 393216
  204.3 77.5 %all-gather.6.cloned.1.call-start = ((), (), s32[]{:S(2)}) async-start(), calls=%async_computation.5 | async-start | bytes 1179648 | tf_op jit(solution)/shard_map/all_gather | solution.py:59
  229.1 849.5 %all-gather.8.cloned.1.call-start = ((), (), s32[]{:S(2)}) async-start(), calls=%async_computation.7 | async-start | bytes 67371008 | tf_op jit(solution)/shard_map/all_gather | solution.py:51
  230.3 0.7 copy-start.2
  231.0 912.8 %reduce-scatter.8.cloned.1.call-start = ((), (), s32[]{:S(2)}) async-start(), calls=%async_computation.6 | async-start | bytes 2228224 | tf_op jit(solution)/shard_map/reduce_scatter | solution.py:68
  1078.5 65.3 %copy-start.1 = (bf16[256,256]{1,0:T(8,128)(2,1)S(1)}, bf16[256,256]{1,0:T(8,128)(2,1)}, u32[]{:S(2)}) copy-start(bf16[256,256]{1,0:T(8,128)(2,1)} %param.12) | copy-start | bytes 393220
Sparse Core Ops, SparseCore 0:
  9.8 42.6 all-gather.3
  127.9 74.3 reduce-scatter.5
  205.0 15.3 reduce-scatter.9
  229.2 52.6 all-gather.5
  283.6 794.8 all-gather.7
  1081.5 62.2 reduce-scatter.7
